TPU v7x, 128 devices: a whole 4x4x4 slice. The times are simulated.
128 devices in a mesh: row: 8 (over z_hi, x), blk: 16 (over z_lo, y, core).
Axes of the slice: x: 4, y: 4, z: 4 (z_hi: 2, z_lo: 2; z = z_hi * 2 + z_lo), core: 2. Of those that a mesh axis runs over, the one named last changes fastest.
Arguments:
- spike_counts: int32 [16384, 2048], P(('row', 'blk')), may hold values from 0 to 23, as said below
- kernel_taps: int32 [16], replicated, may hold values from 1 to 8
- lag_bins: int32 [2], replicated, may hold values from 1 to 32, as said below
Outputs:
- correlogram: bfloat16 [2, 16384, 8, 2048], P(None, 'row', None, 'blk')
Inputs may be any that keep to these rules, and one draw needn't show every extreme that they name: `spike_counts`: neurons fire at different rates and share a common drive. `lag_bins`: the second lag equals 32; the first lies between 1 and 31.
All inputs are finite; a program needn't handle non-finite values.
Results may differ from a plain program's by a relative error of at most 0.0034.
Values may be sent and summed in bfloat16 or wider, within the bound.
A program may use at most 128 MiB of HBM per device.

v0:
```python
import jax
import jax.numpy as jnp
from jax import lax
from jax.sharding import PartitionSpec as P

NEURONS = 16384
BINS = 2048
TAPS = 16


def smoothed(spike_counts, kernel_taps):
    counts = spike_counts.astype(jnp.float32)
    weights = kernel_taps.astype(jnp.float32) / jnp.sum(kernel_taps.astype(jnp.float32))
    padded = jnp.pad(counts, ((0, 0), (TAPS - 1, 0)))
    result = jnp.zeros_like(counts)
    for delay in range(TAPS):
        result = result + weights[delay] * padded[:, TAPS - 1 - delay : TAPS - 1 - delay + BINS]
    return result


def later_bins(data, lag):
    padded = jnp.pad(data, ((0, 0), (0, BINS)))
    return lax.dynamic_slice_in_dim(padded, lag, BINS, 1)


def shards(spike_counts, kernel_taps, lag_bins):
    smooth = smoothed(spike_counts, kernel_taps)
    centred = smooth - jnp.mean(smooth, axis=1, keepdims=True)
    totals = lax.psum(jnp.sum(centred, axis=0), ("row", "blk"))
    residual_part = centred - (totals / NEURONS)[None, :]
    zscored = (
        residual_part
        * lax.rsqrt(jnp.mean(residual_part * residual_part, axis=1, keepdims=True) + 1e-05)
    ).astype(jnp.bfloat16)
    span_rows = zscored.shape[0]
    groups = lax.axis_size("row")
    columns = lax.all_gather(zscored, "row", axis=0, tiled=True)
    stacked = jnp.concatenate(
        [later_bins(columns, lag_bins[0]), later_bins(columns, lag_bins[1])], axis=0
    )
    piece = lax.all_gather(zscored, "blk", axis=0, tiled=True)
    product = jnp.dot(piece, stacked.T, preferred_element_type=jnp.float32) / BINS
    product = product.reshape(piece.shape[0], 2, groups, span_rows)
    return jnp.transpose(product, (1, 0, 2, 3)).astype(jnp.bfloat16)


def solution(mesh):
    placed = (P(("row", "blk"), None), P(), P())
    return jax.shard_map(
        shards, mesh=mesh, in_specs=placed, out_specs=P(None, "row", None, "blk"), check_vma=False
    )
```

profile of v0, /device:TPU:1, one launch (start us, length us, event | category | flops | bytes accessed | tf_op | source)
XLA Modules:
  0.0 258.9 jit_solution(15566849793997691235)
XLA Ops:
  6.5 0.0 copy-start
  6.5 0.0 all-gather.5.cloned.1.call-start
  6.5 1.3 convert_reduce_fusion
  7.8 1.3 convert_divide_fusion
  9.1 0.7 fusion.8
  9.8 1.3 convert_element_type.25
  11.2 14.1 %fusion.6 = (f32[128]{0:T(128)S(1)}, f32[128,2048]{1,0:T(8,128)S(1)}) fusion(f32[]{:T(128)} %bitcast.15, f32[]{:T(128)} %bitcast.14, f32[]{:T(128)} %bitcast.13, f32[]{:T(128)} %bitcast.12, f32[]{:T(128)} %bitcast.11, f32[]{:T(128)} %bitcast.10, f32[]{:T(128)} %bitcast.9, f32[]{:T(128)} %bitcast.8, f32[]{:T(128)} %bitcast.7, f32[]{:T(128)} %bitcast.6, ...), kind=kLoop, calls=%fused_computation.19 | loop fusion | flops 8388480 | bytes 2097728 | tf_op jit(solution)/shard_map/reduce_sum | solution.py:28
  25.3 0.2 subtract_reduce_fusion
  25.5 68.7 %psum.7 = f32[2048]{0:T(1024)S(1)} all-reduce(f32[2048]{0:T(1024)S(1)} %subtract_reduce_fusion), channel_id=1, replica_groups=mesh['row'=8,'blk'=16] {'row','blk'}, use_global_device_ids=true, to_apply=%region_3.4 | all-reduce | flops 2048 | bytes 16384 | tf_op jit(solution)/shard_map/psum | solution.py:29
  94.2 0.3 multiply_reduce_fusion
  94.5 1.0 multiply_convert_fusion.1
  95.5 0.0 all-gather.5.cloned.1.call-update
  95.6 0.2 all-gather.3.cloned.1.call-start
  95.8 0.5 all-gather.3.cloned.1.call-update
  96.3 0.0 copy-done
  96.3 0.6 fusion.7
  100.7 62.5 %all-gather.5.cloned.1.call-done = bf16[1024,2048]{1,0:T(8,128)(2,1)} async-done(((bf16[128,2048]{1,0:T(8,128)(2,1)}), bf16[1024,2048]{1,0:T(8,128)(2,1)}) %all-gather.5.cloned.1.call-update) | async-done | bytes 4194320 | tf_op jit(solution)/shard_map/all_gather | solution.py:37
  163.2 10.0 %pad_dynamic-slice_fusion.1 = (bf16[1024,2048]{1,0:T(8,128)(2,1)}, bf16[1024,2048]{1,0:T(8,128)(2,1)}) fusion(s32[]{:T(128)S(6)} %select_n.6, bf16[1024,2048]{1,0:T(8,128)(2,1)} %all-gather.5.cloned.1.call-done, s32[]{:T(128)S(6)} %select_n.7), kind=kLoop, calls=%fused_computation.2 | loop fusion | bytes 12582920 | tf_op jit(solution)/shard_map/dynamic_slice | solution.py:23
  173.2 42.5 %all-gather.3.cloned.1.call-done = bf16[2048,2048]{1,0:T(8,128)(2,1)} async-done(((bf16[128,2048]{1,0:T(8,128)(2,1)}), bf16[2048,2048]{1,0:T(8,128)(2,1)}) %all-gather.3.cloned.1.call-update) | async-done | bytes 8388624 | tf_op jit(solution)/shard_map/all_gather | solution.py:41
  215.7 23.8 %multiply_convert_fusion = bf16[2048,2048]{0,1:T(8,128)(2,1)} fusion(bf16[2048,2048]{1,0:T(8,128)(2,1)} %all-gather.3.cloned.1.call-done, bf16[1024,2048]{1,0:T(8,128)(2,1)} %get-tuple-element.8, bf16[1024,2048]{1,0:T(8,128)(2,1)} %get-tuple-element.7), kind=kOutput, calls=%fused_computation | convolution fusion | flops 17205035008 | bytes 25165824 | tf_op jit(solution)/shard_map/dot_general | solution.py:42
  239.5 12.6 %copy.4 = bf16[2048,2,8,128]{3,2,0,1:T(8,128)(2,1)} copy(bf16[2048,2,8,128]{0,3,2,1:T(8,128)(2,1)} %bitcast.21) | data formatting | bytes 16777216 | tf_op jit(solution)/shard_map/convert_element_type | solution.py:44
  (3 shorter events, 0.0 us)
Async XLA Ops:
  6.5 89.8 %copy-start = (s32[2]{0:T(128)S(1)}, s32[2]{0:T(128)}, u32[]{:S(2)}) copy-start(s32[2]{0:T(128)} %param.5) | copy-start | bytes 28
  6.5 156.7 %all-gather.5.cloned.1.call-start = ((), (), s32[]{:S(2)}) async-start(), calls=%async_computation.1 | async-start | bytes 4718592 | tf_op jit(solution)/shard_map/all_gather | solution.py:37
  95.6 120.2 %all-gather.3.cloned.1.call-start = ((), (), s32[]{:S(2)}) async-start(), calls=%async_computation | async-start | bytes 8912896 | tf_op jit(solution)/shard_map/all_gather | solution.py:41
Sparse Core Ops, SparseCore 0:
  95.7 67.5 all-gather.4
  165.0 50.7 all-gather.2
where the time goes:
time: 260 us; the launch traced here: 259 us
  waiting for transfers between devices  106 us (41%)
  blocking collectives  68.7 us (26%)
  local copies, waits for them, and re-layouts  23.9 us (9%)
  matrix products  23.8 us (9%)
  other arithmetic  19.5 us (8%)
  between operations  17.2 us (7%)
    psum x1, blocking collectives, shards(): totals = lax.psum(jnp.sum(centred, axis=0), ('row', 'blk'))  68.7 us
    all_gather x1, waiting for transfers between devices, shards(): columns = lax.all_gather(zscored, 'row', axis=0, tiled=True)  62.5 us
    all_gather x1, waiting for transfers between devices, shards(): piece = lax.all_gather(zscored, 'blk', axis=0, tiled=True)  42.5 us
    dot_general x1, matrix products, shards(): jnp.dot(piece, stacked.T, preferred_element_type=jnp.float32) / BINS  23.8 us
    reduce_sum x1, other arithmetic, shards(): centred = smooth - jnp.mean(smooth, axis=1, keepdims=True)  14.1 us
    convert_element_type x1, local copies, waits for them, and re-layouts, shards(): return jnp.transpose(product, (1, 0, 2, 3)).astype(jnp.bfloat16)  12.6 us
    dynamic_slice x1, local copies, waits for them, and re-layouts, later_bins(): return lax.dynamic_slice_in_dim(padded, lag, BINS, 1)  9.97 us
  transfers between devices with their start and end apart: 2, of which 2 were waited for; matrix products, arithmetic and copies ran while one was open for 4% of the time, Pallas kernels for 0%

commit v1 on v0

--- a/solution.py
+++ b/solution.py
@@ -34,7 +34,9 @@
     ).astype(jnp.bfloat16)
     span_rows = zscored.shape[0]
     groups = lax.axis_size("row")
-    columns = lax.all_gather(zscored, "row", axis=0, tiled=True)
+    columns = jnp.concatenate(
+        lax.all_to_all(jnp.stack([zscored] * lax.axis_size("row")), "row", 0, 0), axis=0
+    )
     stacked = jnp.concatenate(
         [later_bins(columns, lag_bins[0]), later_bins(columns, lag_bins[1])], axis=0
     )

time: 260 us -> 234 us (0.900)
  waiting for transfers between devices: 106 us -> 71.5 us
  starting transfers between devices: 0.22 us -> 4.84 us
  local copies, waits for them, and re-layouts: 23.9 us -> 27.4 us
    all_gather x1 -> x0, waiting for transfers between devices: 62.5 us -> none  [shards(): columns = lax.all_gather(zscored, 'row', axis=0, tiled=True)]
    all_to_all x0 -> x1, waiting for transfers between devices: none -> 55.8 us  [shards(): lax.all_to_all(jnp.stack([zscored] * lax.axis_size('row')), 'row', 0, 0)]
    all_gather x1, waiting for transfers between devices: 42.5 us -> 15.7 us  [shards(): piece = lax.all_gather(zscored, 'blk', axis=0, tiled=True)]
    all_to_all x0 -> x1, starting transfers between devices: none -> 4.83 us  [shards(): lax.all_to_all(jnp.stack([zscored] * lax.axis_size('row')), 'row', 0, 0)]
    another operation x0 -> x1, local copies, waits for them, and re-layouts: none -> 3.58 us  [shards(): jnp.stack([zscored] * lax.axis_size('row'))]
  transfers between devices with their start and end apart: 2 -> 2, of which waited for: 2 -> 2; matrix products, arithmetic and copies ran while one was open for 4% -> 6% of each run, Pallas kernels for 0% -> 0%
where the time goes in v1:
time: 234 us; the launch traced here: 233 us
  waiting for transfers between devices  71.5 us (31%)
  blocking collectives  68.7 us (29%)
  local copies, waits for them, and re-layouts  27.4 us (12%)
  matrix products  23.8 us (10%)
  other arithmetic  19.5 us (8%)
  between operations  17 us (7%)
  starting transfers between devices  4.84 us (2%)
    psum x1, blocking collectives, shards(): totals = lax.psum(jnp.sum(centred, axis=0), ('row', 'blk'))  68.7 us
    all_to_all x1, waiting for transfers between devices, shards(): lax.all_to_all(jnp.stack([zscored] * lax.axis_size('row')), 'row', 0, 0)  55.8 us
    dot_general x1, matrix products, shards(): jnp.dot(piece, stacked.T, preferred_element_type=jnp.float32) / BINS  23.8 us
    all_gather x1, waiting for transfers between devices, shards(): piece = lax.all_gather(zscored, 'blk', axis=0, tiled=True)  15.7 us
    reduce_sum x1, other arithmetic, shards(): centred = smooth - jnp.mean(smooth, axis=1, keepdims=True)  14.1 us
    convert_element_type x1, local copies, waits for them, and re-layouts, shards(): return jnp.transpose(product, (1, 0, 2, 3)).astype(jnp.bfloat16)  12.6 us
    dynamic_slice x1, local copies, waits for them, and re-layouts, later_bins(): return lax.dynamic_slice_in_dim(padded, lag, BINS, 1)  9.97 us
    all_to_all x1, starting transfers between devices, shards(): lax.all_to_all(jnp.stack([zscored] * lax.axis_size('row')), 'row', 0, 0)  4.83 us
  transfers between devices with their start and end apart: 2, of which 2 were waited for; matrix products, arithmetic and copies ran while one was open for 6% of the time, Pallas kernels for 0%

profile of v1, /device:TPU:1, one launch (start us, length us, event | category | flops | bytes accessed | tf_op | source)
XLA Modules:
  0.0 232.8 jit_solution(14180848419307631503)
XLA Ops:
  6.5 0.0 all-gather.2.cloned.1.call-start
  6.5 1.3 convert_reduce_fusion
  7.8 1.3 convert_divide_fusion
  9.1 0.7 fusion.8
  9.8 1.3 convert_element_type.25
  11.1 14.1 %fusion.6 = (f32[128]{0:T(128)S(1)}, f32[128,2048]{1,0:T(8,128)S(1)}) fusion(f32[]{:T(128)} %bitcast.15, f32[]{:T(128)} %bitcast.14, f32[]{:T(128)} %bitcast.13, f32[]{:T(128)} %bitcast.12, f32[]{:T(128)} %bitcast.11, f32[]{:T(128)} %bitcast.10, f32[]{:T(128)} %bitcast.9, f32[]{:T(128)} %bitcast.8, f32[]{:T(128)} %bitcast.7, f32[]{:T(128)} %bitcast.6, ...), kind=kLoop, calls=%fused_computation.19 | loop fusion | flops 8388480 | bytes 2097728 | tf_op jit(solution)/shard_map/reduce_sum | solution.py:28
  25.3 0.2 subtract_reduce_fusion
  25.4 0.0 copy-start
  25.5 68.7 %psum.7 = f32[2048]{0:T(1024)S(1)} all-reduce(f32[2048]{0:T(1024)S(1)} %subtract_reduce_fusion), channel_id=1, replica_groups=mesh['row'=8,'blk'=16] {'row','blk'}, use_global_device_ids=true, to_apply=%region_3.4 | all-reduce | flops 2048 | bytes 16384 | tf_op jit(solution)/shard_map/psum | solution.py:29
  94.2 0.3 multiply_reduce_fusion
  94.5 1.0 multiply_convert_fusion.1
  95.5 0.0 all-gather.2.cloned.1.call-update
  95.6 3.6 %stack.2 = bf16[8,128,2048]{2,1,0:T(8,128)(2,1)} broadcast(bf16[128,2048]{1,0:T(8,128)(2,1)} %multiply_convert_fusion.1), dimensions={1,2} | broadcast | bytes 4718592 | tf_op jit(solution)/shard_map/stack | solution.py:38
  99.1 4.8 %all-to-all-start = ((bf16[8,128,2048]{2,1,0:T(8,128)(2,1)}), bf16[8,128,2048]{2,1,0:T(8,128)(2,1)}, u32[]{:S(2)}, u32[]{:S(2)}) async-start(bf16[8,128,2048]{2,1,0:T(8,128)(2,1)} %stack.2), calls=%async_computation | async-start | bytes 8388608 | tf_op jit(solution)/shard_map/all_to_all | solution.py:38
  104.0 0.0 copy-done
  104.0 0.6 fusion.7
  108.1 55.8 %all-to-all-done = bf16[8,128,2048]{2,1,0:T(8,128)(2,1)} async-done(((bf16[8,128,2048]{2,1,0:T(8,128)(2,1)}), bf16[8,128,2048]{2,1,0:T(8,128)(2,1)}, u32[]{:S(2)}, u32[]{:S(2)}) %all-to-all-start) | async-done | bytes 4194336 | tf_op jit(solution)/shard_map/all_to_all | solution.py:38
  163.9 10.0 %pad_dynamic-slice_fusion.1 = (bf16[1024,2048]{1,0:T(8,128)(2,1)}, bf16[1024,2048]{1,0:T(8,128)(2,1)}) fusion(s32[]{:T(128)S(6)} %select_n.6, bf16[1024,2048]{1,0:T(8,128)(2,1)} %bitcast.16, s32[]{:T(128)S(6)} %select_n.7), kind=kLoop, calls=%fused_computation.2 | loop fusion | bytes 12582920 | tf_op jit(solution)/shard_map/dynamic_slice | solution.py:23
  173.9 15.7 %all-gather.2.cloned.1.call-done = bf16[2048,2048]{1,0:T(8,128)(2,1)} async-done(((bf16[128,2048]{1,0:T(8,128)(2,1)}), bf16[2048,2048]{1,0:T(8,128)(2,1)}) %all-gather.2.cloned.1.call-update) | async-done | bytes 8388624 | tf_op jit(solution)/shard_map/all_gather | solution.py:43
  189.6 23.8 %multiply_convert_fusion = bf16[2048,2048]{0,1:T(8,128)(2,1)} fusion(bf16[2048,2048]{1,0:T(8,128)(2,1)} %all-gather.2.cloned.1.call-done, bf16[1024,2048]{1,0:T(8,128)(2,1)} %get-tuple-element.8, bf16[1024,2048]{1,0:T(8,128)(2,1)} %get-tuple-element.7), kind=kOutput, calls=%fused_computation | convolution fusion | flops 17205035008 | bytes 25165824 | tf_op jit(solution)/shard_map/dot_general | solution.py:44
  213.4 12.6 %copy.4 = bf16[2048,2,8,128]{3,2,0,1:T(8,128)(2,1)} copy(bf16[2048,2,8,128]{0,3,2,1:T(8,128)(2,1)} %bitcast.22) | data formatting | bytes 16777216 | tf_op jit(solution)/shard_map/convert_element_type | solution.py:46
  (3 shorter events, 0.0 us)
Async XLA Ops:
  6.5 183.1 %all-gather.2.cloned.1.call-start = ((), (), s32[]{:S(2)}) async-start(), calls=%async_computation.1 | async-start | bytes 8912896 | tf_op jit(solution)/shard_map/all_gather | solution.py:43
  25.4 78.5 %copy-start = (s32[2]{0:T(128)S(1)}, s32[2]{0:T(128)}, u32[]{:S(2)}) copy-start(s32[2]{0:T(128)} %param.5) | copy-start | bytes 28
  99.1 64.8 %all-to-all-start = ((bf16[8,128,2048]{2,1,0:T(8,128)(2,1)}), bf16[8,128,2048]{2,1,0:T(8,128)(2,1)}, u32[]{:S(2)}, u32[]{:S(2)}) async-start(bf16[8,128,2048]{2,1,0:T(8,128)(2,1)} %stack.2), calls=%async_computation | async-start | bytes 8388608 | tf_op jit(solution)/shard_map/all_to_all | solution.py:38
Sparse Core Ops, SparseCore 0:
  95.7 93.8 all-gather.1
